TPU v7x, 512 devices: a whole 4x4x16 slice. The times are simulated.
512 devices in a mesh: sub: 16 (over z), leaf: 32 (over y, x, core).
Axes of the slice: x: 4, y: 4, z: 16, core: 2. Of those that a mesh axis runs over, the one named last changes fastest.
Arguments:
- shift: float32 [1], replicated, may hold values from 0.5 to 2
- self_terms: float32 [524288], P(('leaf', 'sub')), may hold values from 1 to 2
- order: int32 [512, 1024], P(('leaf', 'sub')), may hold values from 0 to 1023, each once within a row
- split: int32 [512], P(('leaf', 'sub')), may hold values from 256 to 768
- coupling: bfloat16 [524288, 768], P(('leaf', 'sub')), as said below
- higher: bfloat16 [524288, 512], P(('leaf', 'sub'))
Outputs:
- applied_higher: bfloat16 [524288, 512], P(('leaf', 'sub'))
Inputs may be any that keep to these rules, and one draw needn't show every extreme that they name: `coupling`: at every node of every level, the symmetric matrix made of diag and the blocks U V^T and V U^T of this and lower levels is positive definite.
All inputs are finite; a program needn't handle non-finite values.
Results may differ from a plain program's by a relative error of at most 0.001.
The roundings to bfloat16 on the way count: a program that leaves them out, or rounds other values in their place, can miss the bound.
Values sent between devices are 32-bit elements; how exact they have to be, the bound alone decides.
A program may use at most 64 MiB of HBM per device.

v0:
```python
import jax
import jax.numpy as jnp
from jax import lax
from jax.sharding import PartitionSpec as P

RANK = 128


def from_partner(value, axis, stride):
    mask = 2**stride
    pairs = [(source, source ^ mask) for source in range(lax.axis_size(axis))]
    return lax.ppermute(value, axis, pairs)


def factor_solve(factor, target):
    lower_part = lax.linalg.triangular_solve(factor, target, left_side=True, lower=True)
    return lax.linalg.triangular_solve(
        factor, lower_part, left_side=True, lower=True, transpose_a=True
    )


def core_terms(left_sum, right_sum):
    width = left_sum.shape[0]
    first = left_sum[:, :width]
    projected = left_sum[:, width:]
    second = right_sum[:, :width]
    beyond = right_sum[:, width:]
    identity_block = jnp.eye(width, dtype=jnp.float32)
    first_factor = jnp.linalg.cholesky(first)
    first_inverse = factor_solve(first_factor, identity_block)
    schur_factor = jnp.linalg.cholesky(first_inverse - second)
    target = beyond - jnp.dot(second, projected, precision=lax.Precision.HIGHEST)
    back = factor_solve(schur_factor, target) - projected
    across = beyond + jnp.dot(second, back, precision=lax.Precision.HIGHEST)
    return (across, back)


def project_rows(basis, columns):
    return lax.dot_general(
        basis, columns, (((0,), (0,)), ((), ())), preferred_element_type=jnp.float32
    )


def node_step(columns, mine, other, is_left):
    left_sum = jnp.where(is_left, mine, other)
    right_sum = jnp.where(is_left, other, mine)
    across, back = core_terms(left_sum, right_sum)
    coefficient = jnp.where(is_left, -across, back).astype(jnp.bfloat16)
    update = columns[:, RANK:].astype(jnp.float32) + jnp.dot(
        columns[:, :RANK], coefficient, preferred_element_type=jnp.float32
    )
    return update.astype(jnp.bfloat16)


def per_device(shift, self_terms, order, split, coupling, higher):
    sub_bits = lax.axis_size("sub").bit_length() - 1
    diagonal = shift[0] + self_terms
    joined = jnp.concatenate([coupling, higher], axis=1).astype(jnp.float32)
    columns = (joined / diagonal[:, None]).astype(jnp.bfloat16)
    inside = (order[0] < split[0]).astype(jnp.bfloat16)[:, None]
    outside = 1 - inside
    basis = coupling[:, :RANK]
    left_sum = project_rows(basis * inside, columns)
    right_sum = project_rows(basis * outside, columns)
    across, back = core_terms(left_sum, right_sum)
    own = columns[:, :RANK]
    update = columns[:, RANK:].astype(jnp.float32)
    update = update + jnp.dot(
        own * inside, (-across).astype(jnp.bfloat16), preferred_element_type=jnp.float32
    )
    update = update + jnp.dot(
        own * outside, back.astype(jnp.bfloat16), preferred_element_type=jnp.float32
    )
    columns = update.astype(jnp.bfloat16)
    position = lax.axis_index("sub")
    for level in range(1, sub_bits + 1):
        basis = coupling[:, level * RANK : (level + 1) * RANK]
        partial_value = project_rows(basis, columns)
        stride = 2 ** (level - 1)
        mine = partial_value
        for bit in range(level - 1):
            mine = mine + from_partner(mine, "sub", bit)
        other = from_partner(mine, "sub", level - 1)
        is_left = position // stride % 2 == 0
        columns = node_step(columns, mine, other, is_left)
    top = sub_bits + 1
    basis = coupling[:, top * RANK : (top + 1) * RANK]
    partial_value = project_rows(basis, columns)
    mine = lax.psum(partial_value, "sub")
    other = from_partner(mine, "leaf", 0)
    is_left = lax.axis_index("leaf") % 2 == 0
    return node_step(columns, mine, other, is_left)


def solution(mesh):
    in_specs = (
        P(),
        P(("leaf", "sub")),
        P(("leaf", "sub"), None),
        P(("leaf", "sub")),
        P(("leaf", "sub"), None),
        P(("leaf", "sub"), None),
    )
    out_specs = P(("leaf", "sub"), None)
    return jax.shard_map(
        per_device, mesh=mesh, in_specs=in_specs, out_specs=out_specs, check_vma=False
    )
```

profile of v0, /device:TPU:1, one launch (start us, length us, event | category | flops | bytes accessed | tf_op | source)
XLA Modules:
  0.0 782.3 jit_solution(3534729396626597273)
XLA Ops:
  9.2 2.3 divide_convert_fusion
  17.2 11.7 %cholesky.194 = f32[128,128]{1,0:T(8,128)S(1)} custom-call(f32[128,128]{1,0:T(8,128)S(1)} %fusion.114), custom_call_target="Cholesky" | custom-call | tf_op jit(solution)/shard_map/jit(cholesky)/cholesky | solution.py:29
  30.1 9.8 %custom-call.55 = f32[1,128,128]{1,2,0:T(8,128)S(1)} custom-call(f32[1,128,128]{2,1,0:T(8,128)S(1)} %fusion.61), custom_call_target="InvertDiagBlocksLowerTriangular" | custom-call | tf_op jit(solution)/shard_map/triangular_solve/custom-call.2 | solution.py:17
  42.2 11.7 %cholesky.205 = f32[128,128]{1,0:T(8,128)S(1)} custom-call(f32[128,128]{1,0:T(8,128)S(1)} %fusion.111), custom_call_target="Cholesky" | custom-call | tf_op jit(solution)/shard_map/jit(cholesky)/cholesky | solution.py:31
  55.4 9.8 %custom-call.38 = f32[1,128,128]{1,2,0:T(8,128)S(1)} custom-call(f32[1,128,128]{2,1,0:T(8,128)S(1)} %fusion.62), custom_call_target="InvertDiagBlocksLowerTriangular" | custom-call | tf_op jit(solution)/shard_map/triangular_solve | solution.py:17
  73.0 4.4 collective-permute-start
  77.4 8.5 %collective-permute-done = f32[128,1152]{0,1:T(8,128)S(1)} collective-permute-done((f32[128,1152]{0,1:T(8,128)S(1)}, f32[128,1152]{0,1:T(8,128)S(1)}, u32[]{:S(2)}, u32[]{:S(2)}) %collective-permute-start) | collective-permute-done | bytes 589856 | tf_op jit(solution)/shard_map/ppermute | solution.py:12
  86.1 11.7 %cholesky.216 = f32[128,128]{1,0:T(8,128)S(1)} custom-call(f32[128,128]{1,0:T(8,128)S(1)} %fusion.107), custom_call_target="Cholesky" | custom-call | tf_op jit(solution)/shard_map/jit(cholesky)/cholesky | solution.py:29
  99.2 9.8 %custom-call.57 = f32[1,128,128]{1,2,0:T(8,128)S(1)} custom-call(f32[1,128,128]{2,1,0:T(8,128)S(1)} %fusion.63), custom_call_target="InvertDiagBlocksLowerTriangular" | custom-call | tf_op jit(solution)/shard_map/triangular_solve/custom-call.2 | solution.py:17
  110.3 11.7 %cholesky.227 = f32[128,128]{1,0:T(8,128)S(1)} custom-call(f32[128,128]{1,0:T(8,128)S(1)} %fusion.104), custom_call_target="Cholesky" | custom-call | tf_op jit(solution)/shard_map/jit(cholesky)/cholesky | solution.py:31
  123.3 21.7 %custom-call.39 = f32[1,128,128]{1,2,0:T(8,128)S(1)} custom-call(f32[1,128,128]{2,1,0:T(8,128)S(1)} %fusion.64), custom_call_target="InvertDiagBlocksLowerTriangular" | custom-call | tf_op jit(solution)/shard_map/triangular_solve | solution.py:17
  147.3 2.4 add_convert_fusion
  151.0 4.1 collective-permute-start.1
  155.1 7.0 collective-permute-done.1
  162.2 12.1 %collective-permute-start.2 = (f32[128,1024]{0,1:T(8,128)S(1)}, f32[128,1024]{0,1:T(8,128)}, u32[]{:S(2)}, u32[]{:S(2)}) collective-permute-start(f32[128,1024]{0,1:T(8,128)S(1)} %add.127), channel_id=1, source_target_pairs={{0,64},{32,96},{64,0},{96,32},{128,192},{160,224},{192,128},{224,1... | collective-permute-start | bytes 1572872 | tf_op jit(solution)/shard_map/ppermute | solution.py:12
  174.4 22.8 %collective-permute-done.2 = f32[128,1024]{0,1:T(8,128)} collective-permute-done((f32[128,1024]{0,1:T(8,128)S(1)}, f32[128,1024]{0,1:T(8,128)}, u32[]{:S(2)}, u32[]{:S(2)}) %collective-permute-start.2) | collective-permute-done | bytes 524320 | tf_op jit(solution)/shard_map/ppermute | solution.py:12
  198.5 11.7 %cholesky.238 = f32[128,128]{1,0:T(8,128)S(1)} custom-call(f32[128,128]{1,0:T(8,128)S(1)} %fusion.100), custom_call_target="Cholesky" | custom-call | tf_op jit(solution)/shard_map/jit(cholesky)/cholesky | solution.py:29
  211.6 9.8 %custom-call.59 = f32[1,128,128]{1,2,0:T(8,128)S(1)} custom-call(f32[1,128,128]{2,1,0:T(8,128)S(1)} %fusion.65), custom_call_target="InvertDiagBlocksLowerTriangular" | custom-call | tf_op jit(solution)/shard_map/triangular_solve/custom-call.2 | solution.py:17
  222.6 11.7 %cholesky.249 = f32[128,128]{1,0:T(8,128)S(1)} custom-call(f32[128,128]{1,0:T(8,128)S(1)} %fusion.97), custom_call_target="Cholesky" | custom-call | tf_op jit(solution)/shard_map/jit(cholesky)/cholesky | solution.py:31
  235.7 10.2 %custom-call.40 = f32[1,128,128]{1,2,0:T(8,128)S(1)} custom-call(f32[1,128,128]{2,1,0:T(8,128)S(1)} %fusion.66), custom_call_target="InvertDiagBlocksLowerTriangular" | custom-call | tf_op jit(solution)/shard_map/triangular_solve | solution.py:17
  247.9 2.2 add_convert_fusion.1
  250.9 2.9 collective-permute-start.3
  253.8 9.7 %collective-permute-done.3 = f32[128,896]{0,1:T(8,128)S(1)} collective-permute-done((f32[128,896]{0,1:T(8,128)S(1)}, f32[128,896]{0,1:T(8,128)S(1)}, u32[]{:S(2)}, u32[]{:S(2)}) %collective-permute-start.3) | collective-permute-done | bytes 458784 | tf_op jit(solution)/shard_map/ppermute | solution.py:12
  263.6 5.7 collective-permute-start.4
  269.3 19.9 %collective-permute-done.4 = f32[128,896]{0,1:T(8,128)S(1)} collective-permute-done((f32[128,896]{0,1:T(8,128)S(1)}, f32[128,896]{0,1:T(8,128)S(1)}, u32[]{:S(2)}, u32[]{:S(2)}) %collective-permute-start.4) | collective-permute-done | bytes 458784 | tf_op jit(solution)/shard_map/ppermute | solution.py:12
  289.3 8.8 %collective-permute-start.5 = (f32[128,896]{0,1:T(8,128)S(1)}, f32[128,896]{0,1:T(8,128)S(1)}, u32[]{:S(2)}, u32[]{:S(2)}) collective-permute-start(f32[128,896]{0,1:T(8,128)S(1)} %add.132), channel_id=1, source_target_pairs={{0,128},{32,160},{64,192},{96,224},{128,0},{160,32},{192,64},{224,... | collective-permute-start | bytes 1376264 | tf_op jit(solution)/shard_map/ppermute | solution.py:12
  298.1 39.4 %collective-permute-done.5 = f32[128,896]{0,1:T(8,128)S(1)} collective-permute-done((f32[128,896]{0,1:T(8,128)S(1)}, f32[128,896]{0,1:T(8,128)S(1)}, u32[]{:S(2)}, u32[]{:S(2)}) %collective-permute-start.5) | collective-permute-done | bytes 458784 | tf_op jit(solution)/shard_map/ppermute | solution.py:12
  337.7 11.7 %cholesky.260 = f32[128,128]{1,0:T(8,128)S(1)} custom-call(f32[128,128]{1,0:T(8,128)S(1)} %fusion.93), custom_call_target="Cholesky" | custom-call | tf_op jit(solution)/shard_map/jit(cholesky)/cholesky | solution.py:29
  350.7 9.8 %custom-call.61 = f32[1,128,128]{1,2,0:T(8,128)S(1)} custom-call(f32[1,128,128]{2,1,0:T(8,128)S(1)} %fusion.67), custom_call_target="InvertDiagBlocksLowerTriangular" | custom-call | tf_op jit(solution)/shard_map/triangular_solve/custom-call.2 | solution.py:17
  361.7 11.7 %cholesky.271 = f32[128,128]{1,0:T(8,128)S(1)} custom-call(f32[128,128]{1,0:T(8,128)S(1)} %fusion.90), custom_call_target="Cholesky" | custom-call | tf_op jit(solution)/shard_map/jit(cholesky)/cholesky | solution.py:31
  374.8 9.9 %custom-call.41 = f32[1,128,128]{1,2,0:T(8,128)S(1)} custom-call(f32[1,128,128]{2,1,0:T(8,128)S(1)} %fusion.68), custom_call_target="InvertDiagBlocksLowerTriangular" | custom-call | tf_op jit(solution)/shard_map/triangular_solve | solution.py:17
  391.2 10.1 %collective-permute-done.6 = f32[128,768]{0,1:T(8,128)S(1)} collective-permute-done((f32[128,768]{0,1:T(8,128)S(1)}, f32[128,768]{0,1:T(8,128)S(1)}, u32[]{:S(2)}, u32[]{:S(2)}) %collective-permute-start.6) | collective-permute-done | bytes 393248 | tf_op jit(solution)/shard_map/ppermute | solution.py:12
  403.3 20.3 %collective-permute-done.7 = f32[128,768]{0,1:T(8,128)S(1)} collective-permute-done((f32[128,768]{0,1:T(8,128)S(1)}, f32[128,768]{0,1:T(8,128)S(1)}, u32[]{:S(2)}, u32[]{:S(2)}) %collective-permute-start.7) | collective-permute-done | bytes 393248 | tf_op jit(solution)/shard_map/ppermute | solution.py:12
  423.7 4.3 collective-permute-start.8
  428.0 35.9 %collective-permute-done.8 = f32[128,768]{0,1:T(8,128)S(1)} collective-permute-done((f32[128,768]{0,1:T(8,128)S(1)}, f32[128,768]{0,1:T(8,128)S(1)}, u32[]{:S(2)}, u32[]{:S(2)}) %collective-permute-start.8) | collective-permute-done | bytes 393248 | tf_op jit(solution)/shard_map/ppermute | solution.py:12
  464.7 19.0 %collective-permute-start.9 = (f32[128,768]{0,1:T(8,128)}, f32[128,768]{0,1:T(8,128)}, u32[]{:S(2)}, u32[]{:S(2)}) collective-permute-start(f32[128,768]{0,1:T(8,128)} %add.138), channel_id=1, source_target_pairs={{0,256},{32,288},{64,320},{96,352},{128,384},{160,416},{192,448},{... | collective-permute-start | bytes 1179656 | tf_op jit(solution)/shard_map/ppermute | solution.py:12
  483.7 14.6 %collective-permute-done.9 = f32[128,768]{0,1:T(8,128)} collective-permute-done((f32[128,768]{0,1:T(8,128)}, f32[128,768]{0,1:T(8,128)}, u32[]{:S(2)}, u32[]{:S(2)}) %collective-permute-start.9) | collective-permute-done | bytes 393248 | tf_op jit(solution)/shard_map/ppermute | solution.py:12
  503.9 13.2 %cholesky.282 = f32[128,128]{1,0:T(8,128)} custom-call(f32[128,128]{1,0:T(8,128)} %fusion.86), custom_call_target="Cholesky" | custom-call | tf_op jit(solution)/shard_map/jit(cholesky)/cholesky | solution.py:29
  520.7 11.3 %custom-call.63 = f32[1,128,128]{1,2,0:T(8,128)} custom-call(f32[1,128,128]{2,1,0:T(8,128)} %fusion.69), custom_call_target="InvertDiagBlocksLowerTriangular" | custom-call | tf_op jit(solution)/shard_map/triangular_solve/custom-call.2 | solution.py:17
  540.1 13.2 %cholesky.293 = f32[128,128]{1,0:T(8,128)} custom-call(f32[128,128]{1,0:T(8,128)} %fusion.83), custom_call_target="Cholesky" | custom-call | tf_op jit(solution)/shard_map/jit(cholesky)/cholesky | solution.py:31
  556.9 11.4 %custom-call.42 = f32[1,128,128]{1,2,0:T(8,128)} custom-call(f32[1,128,128]{2,1,0:T(8,128)} %fusion.70), custom_call_target="InvertDiagBlocksLowerTriangular" | custom-call | tf_op jit(solution)/shard_map/triangular_solve | solution.py:17
  575.8 133.2 %all-reduce.2.cloned.1.call-done = f32[128,640]{0,1:T(8,128)} async-done(((f32[128,640]{0,1:T(8,128)}), f32[128,640]{0,1:T(8,128)}) %all-reduce.2.cloned.1.call-update) | async-done | bytes 327696 | tf_op jit(solution)/shard_map/psum | solution.py:89
  708.9 12.3 %collective-permute-start.10 = (f32[128,640]{0,1:T(8,128)}, f32[128,640]{0,1:T(8,128)S(1)}, u32[]{:S(2)}, u32[]{:S(2)}) collective-permute-start(f32[128,640]{0,1:T(8,128)} %all-reduce.2.cloned.1.call-done), channel_id=1, source_target_pairs={{0,1},{1,0},{2,3},{3,2},{4,5},{5,4},{6,7},{7,6},{8,9},{9,8},{10,11... | collective-permute-start | bytes 983048 | tf_op jit(solution)/shard_map/ppermute | solution.py:12
  723.9 11.7 %cholesky.304 = f32[128,128]{1,0:T(8,128)S(1)} custom-call(f32[128,128]{1,0:T(8,128)S(1)} %fusion.79), custom_call_target="Cholesky" | custom-call | tf_op jit(solution)/shard_map/jit(cholesky)/cholesky | solution.py:29
  736.9 9.8 %custom-call.65 = f32[1,128,128]{1,2,0:T(8,128)S(1)} custom-call(f32[1,128,128]{2,1,0:T(8,128)S(1)} %fusion.71), custom_call_target="InvertDiagBlocksLowerTriangular" | custom-call | tf_op jit(solution)/shard_map/triangular_solve/custom-call.2 | solution.py:17
  747.8 11.7 %cholesky.315 = f32[128,128]{1,0:T(8,128)S(1)} custom-call(f32[128,128]{1,0:T(8,128)S(1)} %fusion.76), custom_call_target="Cholesky" | custom-call | tf_op jit(solution)/shard_map/jit(cholesky)/cholesky | solution.py:31
  760.9 10.0 %custom-call.43 = f32[1,128,128]{1,2,0:T(8,128)S(1)} custom-call(f32[1,128,128]{2,1,0:T(8,128)S(1)} %fusion.72), custom_call_target="InvertDiagBlocksLowerTriangular" | custom-call | tf_op jit(solution)/shard_map/triangular_solve | solution.py:17
  772.3 2.7 add_convert_fusion.4
  (146 shorter events, 84.4 us)
Async XLA Ops:
  6.5 702.4 %all-reduce.2.cloned.1.call-start = ((), (), s32[]{:S(2)}) async-start(), calls=%async_computation | async-start | bytes 655360 | tf_op jit(solution)/shard_map/psum | solution.py:89
  14.8 0.8 copy-start.5
  71.0 2.0 copy-start
  73.0 12.9 %collective-permute-start = (f32[128,1152]{0,1:T(8,128)S(1)}, f32[128,1152]{0,1:T(8,128)S(1)}, u32[]{:S(2)}, u32[]{:S(2)}) collective-permute-start(f32[128,1152]{0,1:T(8,128)S(1)} %convolution_bitcast_fusion), channel_id=1, source_target_pairs={{0,32},{32,0},{64,96},{96,64},{128,160},{160,128},{192,224},{224,1... | collective-permute-start | bytes 1769480 | tf_op jit(solution)/shard_map/ppermute | solution.py:12
  146.7 3.0 copy-start.1
  149.7 1.4 copy-start.2
  151.0 11.1 %collective-permute-start.1 = (f32[128,1024]{0,1:T(8,128)S(1)}, f32[128,1024]{0,1:T(8,128)S(1)}, u32[]{:S(2)}, u32[]{:S(2)}) collective-permute-start(f32[128,1024]{0,1:T(8,128)S(1)} %convolution_bitcast_fusion.1), channel_id=1, source_target_pairs={{0,32},{32,0},{64,96},{96,64},{128,160},{160,128},{192,224},{224,1... | collective-permute-start | bytes 1572872 | tf_op jit(solution)/shard_map/ppermute | solution.py:12
  162.2 35.0 %collective-permute-start.2 = (f32[128,1024]{0,1:T(8,128)S(1)}, f32[128,1024]{0,1:T(8,128)}, u32[]{:S(2)}, u32[]{:S(2)}) collective-permute-start(f32[128,1024]{0,1:T(8,128)S(1)} %add.127), channel_id=1, source_target_pairs={{0,64},{32,96},{64,0},{96,32},{128,192},{160,224},{192,128},{224,1... | collective-permute-start | bytes 1572872 | tf_op jit(solution)/shard_map/ppermute | solution.py:12
  250.2 39.1 %copy-start.3 = (bf16[1024,896]{1,0:T(8,128)(2,1)}, bf16[1024,896]{1,0:T(8,128)(2,1)S(1)}, u32[]{:S(2)}) copy-start(bf16[1024,896]{1,0:T(8,128)(2,1)S(1)} %add_convert_fusion.1) | copy-start | bytes 5505028
  250.9 12.7 %collective-permute-start.3 = (f32[128,896]{0,1:T(8,128)S(1)}, f32[128,896]{0,1:T(8,128)S(1)}, u32[]{:S(2)}, u32[]{:S(2)}) collective-permute-start(f32[128,896]{0,1:T(8,128)S(1)} %convolution_bitcast_fusion.2), channel_id=1, source_target_pairs={{0,32},{32,0},{64,96},{96,64},{128,160},{160,128},{192,224},{224,1... | collective-permute-start | bytes 1376264 | tf_op jit(solution)/shard_map/ppermute | solution.py:12
  263.6 25.6 %collective-permute-start.4 = (f32[128,896]{0,1:T(8,128)S(1)}, f32[128,896]{0,1:T(8,128)S(1)}, u32[]{:S(2)}, u32[]{:S(2)}) collective-permute-start(f32[128,896]{0,1:T(8,128)S(1)} %add.131), channel_id=1, source_target_pairs={{0,64},{32,96},{64,0},{96,32},{128,192},{160,224},{192,128},{224,1... | collective-permute-start | bytes 1376264 | tf_op jit(solution)/shard_map/ppermute | solution.py:12
  289.3 48.2 %collective-permute-start.5 = (f32[128,896]{0,1:T(8,128)S(1)}, f32[128,896]{0,1:T(8,128)S(1)}, u32[]{:S(2)}, u32[]{:S(2)}) collective-permute-start(f32[128,896]{0,1:T(8,128)S(1)} %add.132), channel_id=1, source_target_pairs={{0,128},{32,160},{64,192},{96,224},{128,0},{160,32},{192,64},{224,... | collective-permute-start | bytes 1376264 | tf_op jit(solution)/shard_map/ppermute | solution.py:12
  389.2 12.1 %collective-permute-start.6 = (f32[128,768]{0,1:T(8,128)S(1)}, f32[128,768]{0,1:T(8,128)S(1)}, u32[]{:S(2)}, u32[]{:S(2)}) collective-permute-start(f32[128,768]{0,1:T(8,128)S(1)} %convolution_bitcast_fusion.3), channel_id=1, source_target_pairs={{0,32},{32,0},{64,96},{96,64},{128,160},{160,128},{192,224},{224,1... | collective-permute-start | bytes 1179656 | tf_op jit(solution)/shard_map/ppermute | solution.py:12
  401.4 22.2 %collective-permute-start.7 = (f32[128,768]{0,1:T(8,128)S(1)}, f32[128,768]{0,1:T(8,128)S(1)}, u32[]{:S(2)}, u32[]{:S(2)}) collective-permute-start(f32[128,768]{0,1:T(8,128)S(1)} %add.136), channel_id=1, source_target_pairs={{0,64},{32,96},{64,0},{96,32},{128,192},{160,224},{192,128},{224,1... | collective-permute-start | bytes 1179656 | tf_op jit(solution)/shard_map/ppermute | solution.py:12
  423.7 40.2 %collective-permute-start.8 = (f32[128,768]{0,1:T(8,128)S(1)}, f32[128,768]{0,1:T(8,128)S(1)}, u32[]{:S(2)}, u32[]{:S(2)}) collective-permute-start(f32[128,768]{0,1:T(8,128)S(1)} %add.137), channel_id=1, source_target_pairs={{0,128},{32,160},{64,192},{96,224},{128,0},{160,32},{192,64},{224,... | collective-permute-start | bytes 1179656 | tf_op jit(solution)/shard_map/ppermute | solution.py:12
  464.7 33.7 %collective-permute-start.9 = (f32[128,768]{0,1:T(8,128)}, f32[128,768]{0,1:T(8,128)}, u32[]{:S(2)}, u32[]{:S(2)}) collective-permute-start(f32[128,768]{0,1:T(8,128)} %add.138), channel_id=1, source_target_pairs={{0,256},{32,288},{64,320},{96,352},{128,384},{160,416},{192,448},{... | collective-permute-start | bytes 1179656 | tf_op jit(solution)/shard_map/ppermute | solution.py:12
  573.4 1.1 copy-start.4
  708.9 13.8 %collective-permute-start.10 = (f32[128,640]{0,1:T(8,128)}, f32[128,640]{0,1:T(8,128)S(1)}, u32[]{:S(2)}, u32[]{:S(2)}) collective-permute-start(f32[128,640]{0,1:T(8,128)} %all-reduce.2.cloned.1.call-done), channel_id=1, source_target_pairs={{0,1},{1,0},{2,3},{3,2},{4,5},{5,4},{6,7},{7,6},{8,9},{9,8},{10,11... | collective-permute-start | bytes 983048 | tf_op jit(solution)/shard_map/ppermute | solution.py:12
Sparse Core Ops, SparseCore 0:
  575.9 133.0 all-reduce.1
where the time goes:
time: 793 us; the launch traced here: 782 us
  waiting for transfers between devices  323 us (41%)
  other arithmetic  310 us (39%)
  starting transfers between devices  77.5 us (10%)
  matrix products  48.2 us (6%)
  between operations  16.1 us (2%)
    ppermute x11, waiting for transfers between devices, from_partner(): return lax.ppermute(value, axis, pairs)  190 us
    another operation x24, other arithmetic, factor_solve(): lax.linalg.triangular_solve(factor, lower_part, left_side=True, lower=Tru...  144 us
    psum x1, waiting for transfers between devices, per_device(): mine = lax.psum(partial_value, 'sub')  133 us
    ppermute x11, starting transfers between devices, from_partner(): return lax.ppermute(value, axis, pairs)  77.5 us
    another operation x18, other arithmetic, core_terms(): schur_factor = jnp.linalg.cholesky(first_inverse - second)  76.9 us
    another operation x18, other arithmetic, core_terms(): first_factor = jnp.linalg.cholesky(first)  76.6 us
  transfers between devices with their start and end apart: 12, of which 12 were waited for; matrix products, arithmetic and copies ran while one was open for 0% of the time, Pallas kernels for 0%

commit v1 on v0

--- a/solution.py
+++ b/solution.py
@@ -86,7 +86,7 @@
     top = sub_bits + 1
     basis = coupling[:, top * RANK : (top + 1) * RANK]
     partial_value = project_rows(basis, columns)
-    mine = lax.psum(partial_value, "sub")
+    mine = jnp.sum(lax.all_gather(partial_value, "sub"), axis=0)
     other = from_partner(mine, "leaf", 0)
     is_left = lax.axis_index("leaf") % 2 == 0
     return node_step(columns, mine, other, is_left)

time: 793 us -> 764 us (0.963)
  waiting for transfers between devices: 323 us -> 288 us
    psum x1 -> x0, waiting for transfers between devices: 133 us -> none  [per_device(): mine = lax.psum(partial_value, 'sub')]
    all_gather x0 -> x1, waiting for transfers between devices: none -> 98.2 us  [per_device(): mine = jnp.sum(lax.all_gather(partial_value, 'sub'), axis=0)]
where the time goes in v1:
time: 764 us; the launch traced here: 754 us
  other arithmetic  310 us (41%)
  waiting for transfers between devices  288 us (38%)
  starting transfers between devices  80.3 us (11%)
  matrix products  48.2 us (6%)
  between operations  15.9 us (2%)
  local copies, waits for them, and re-layouts  11.6 us (2%)
    ppermute x11, waiting for transfers between devices, from_partner(): return lax.ppermute(value, axis, pairs)  190 us
    another operation x24, other arithmetic, factor_solve(): lax.linalg.triangular_solve(factor, lower_part, left_side=True, lower=Tru...  144 us
    all_gather x1, waiting for transfers between devices, per_device(): mine = jnp.sum(lax.all_gather(partial_value, 'sub'), axis=0)  98.2 us
    ppermute x11, starting transfers between devices, from_partner(): return lax.ppermute(value, axis, pairs)  80.3 us
    another operation x18, other arithmetic, core_terms(): schur_factor = jnp.linalg.cholesky(first_inverse - second)  77 us
    another operation x18, other arithmetic, core_terms(): first_factor = jnp.linalg.cholesky(first)  76.6 us
  transfers between devices with their start and end apart: 12, of which 12 were waited for; matrix products, arithmetic and copies ran while one was open for 0% of the time, Pallas kernels for 0%

profile of v1, /device:TPU:1, one launch (start us, length us, event | category | flops | bytes accessed | tf_op | source)
XLA Modules:
  0.0 753.8 jit_solution(16596203525799476336)
XLA Ops:
  9.2 2.3 divide_convert_fusion
  17.2 11.7 %cholesky.194 = f32[128,128]{1,0:T(8,128)S(1)} custom-call(f32[128,128]{1,0:T(8,128)S(1)} %fusion.114), custom_call_target="Cholesky" | custom-call | tf_op jit(solution)/shard_map/jit(cholesky)/cholesky | solution.py:29
  30.1 9.8 %custom-call.55 = f32[1,128,128]{1,2,0:T(8,128)S(1)} custom-call(f32[1,128,128]{2,1,0:T(8,128)S(1)} %fusion.61), custom_call_target="InvertDiagBlocksLowerTriangular" | custom-call | tf_op jit(solution)/shard_map/triangular_solve/custom-call.2 | solution.py:17
  42.2 11.7 %cholesky.205 = f32[128,128]{1,0:T(8,128)S(1)} custom-call(f32[128,128]{1,0:T(8,128)S(1)} %fusion.111), custom_call_target="Cholesky" | custom-call | tf_op jit(solution)/shard_map/jit(cholesky)/cholesky | solution.py:31
  55.5 9.8 %custom-call.38 = f32[1,128,128]{1,2,0:T(8,128)S(1)} custom-call(f32[1,128,128]{2,1,0:T(8,128)S(1)} %fusion.62), custom_call_target="InvertDiagBlocksLowerTriangular" | custom-call | tf_op jit(solution)/shard_map/triangular_solve | solution.py:17
  73.1 4.4 collective-permute-start
  77.5 8.5 %collective-permute-done = f32[128,1152]{0,1:T(8,128)S(1)} collective-permute-done((f32[128,1152]{0,1:T(8,128)S(1)}, f32[128,1152]{0,1:T(8,128)S(1)}, u32[]{:S(2)}, u32[]{:S(2)}) %collective-permute-start) | collective-permute-done | bytes 589856 | tf_op jit(solution)/shard_map/ppermute | solution.py:12
  86.3 11.7 %cholesky.216 = f32[128,128]{1,0:T(8,128)S(1)} custom-call(f32[128,128]{1,0:T(8,128)S(1)} %fusion.107), custom_call_target="Cholesky" | custom-call | tf_op jit(solution)/shard_map/jit(cholesky)/cholesky | solution.py:29
  99.4 9.8 %custom-call.57 = f32[1,128,128]{1,2,0:T(8,128)S(1)} custom-call(f32[1,128,128]{2,1,0:T(8,128)S(1)} %fusion.63), custom_call_target="InvertDiagBlocksLowerTriangular" | custom-call | tf_op jit(solution)/shard_map/triangular_solve/custom-call.2 | solution.py:17
  110.4 11.7 %cholesky.227 = f32[128,128]{1,0:T(8,128)S(1)} custom-call(f32[128,128]{1,0:T(8,128)S(1)} %fusion.104), custom_call_target="Cholesky" | custom-call | tf_op jit(solution)/shard_map/jit(cholesky)/cholesky | solution.py:31
  123.5 21.7 %custom-call.39 = f32[1,128,128]{1,2,0:T(8,128)S(1)} custom-call(f32[1,128,128]{2,1,0:T(8,128)S(1)} %fusion.64), custom_call_target="InvertDiagBlocksLowerTriangular" | custom-call | tf_op jit(solution)/shard_map/triangular_solve | solution.py:17
  147.5 2.4 add_convert_fusion
  151.3 4.1 collective-permute-start.1
  155.4 7.0 collective-permute-done.1
  162.5 12.1 %collective-permute-start.2 = (f32[128,1024]{0,1:T(8,128)S(1)}, f32[128,1024]{0,1:T(8,128)}, u32[]{:S(2)}, u32[]{:S(2)}) collective-permute-start(f32[128,1024]{0,1:T(8,128)S(1)} %add.125), channel_id=1, source_target_pairs={{0,64},{32,96},{64,0},{96,32},{128,192},{160,224},{192,128},{224,1... | collective-permute-start | bytes 1572872 | tf_op jit(solution)/shard_map/ppermute | solution.py:12
  174.6 22.9 %collective-permute-done.2 = f32[128,1024]{0,1:T(8,128)} collective-permute-done((f32[128,1024]{0,1:T(8,128)S(1)}, f32[128,1024]{0,1:T(8,128)}, u32[]{:S(2)}, u32[]{:S(2)}) %collective-permute-start.2) | collective-permute-done | bytes 524320 | tf_op jit(solution)/shard_map/ppermute | solution.py:12
  198.8 11.7 %cholesky.238 = f32[128,128]{1,0:T(8,128)S(1)} custom-call(f32[128,128]{1,0:T(8,128)S(1)} %fusion.100), custom_call_target="Cholesky" | custom-call | tf_op jit(solution)/shard_map/jit(cholesky)/cholesky | solution.py:29
  211.8 9.8 %custom-call.59 = f32[1,128,128]{1,2,0:T(8,128)S(1)} custom-call(f32[1,128,128]{2,1,0:T(8,128)S(1)} %fusion.65), custom_call_target="InvertDiagBlocksLowerTriangular" | custom-call | tf_op jit(solution)/shard_map/triangular_solve/custom-call.2 | solution.py:17
  222.9 11.7 %cholesky.249 = f32[128,128]{1,0:T(8,128)S(1)} custom-call(f32[128,128]{1,0:T(8,128)S(1)} %fusion.97), custom_call_target="Cholesky" | custom-call | tf_op jit(solution)/shard_map/jit(cholesky)/cholesky | solution.py:31
  235.9 10.2 %custom-call.40 = f32[1,128,128]{1,2,0:T(8,128)S(1)} custom-call(f32[1,128,128]{2,1,0:T(8,128)S(1)} %fusion.66), custom_call_target="InvertDiagBlocksLowerTriangular" | custom-call | tf_op jit(solution)/shard_map/triangular_solve | solution.py:17
  251.1 2.8 collective-permute-start.3
  253.9 9.9 %collective-permute-done.3 = f32[128,896]{0,1:T(8,128)S(1)} collective-permute-done((f32[128,896]{0,1:T(8,128)S(1)}, f32[128,896]{0,1:T(8,128)S(1)}, u32[]{:S(2)}, u32[]{:S(2)}) %collective-permute-start.3) | collective-permute-done | bytes 458784 | tf_op jit(solution)/shard_map/ppermute | solution.py:12
  263.9 5.5 collective-permute-start.4
  269.4 19.9 %collective-permute-done.4 = f32[128,896]{0,1:T(8,128)S(1)} collective-permute-done((f32[128,896]{0,1:T(8,128)S(1)}, f32[128,896]{0,1:T(8,128)S(1)}, u32[]{:S(2)}, u32[]{:S(2)}) %collective-permute-start.4) | collective-permute-done | bytes 458784 | tf_op jit(solution)/shard_map/ppermute | solution.py:12
  289.4 8.8 %collective-permute-start.5 = (f32[128,896]{0,1:T(8,128)S(1)}, f32[128,896]{0,1:T(8,128)S(1)}, u32[]{:S(2)}, u32[]{:S(2)}) collective-permute-start(f32[128,896]{0,1:T(8,128)S(1)} %add.130), channel_id=1, source_target_pairs={{0,128},{32,160},{64,192},{96,224},{128,0},{160,32},{192,64},{224,... | collective-permute-start | bytes 1376264 | tf_op jit(solution)/shard_map/ppermute | solution.py:12
  298.2 39.4 %collective-permute-done.5 = f32[128,896]{0,1:T(8,128)S(1)} collective-permute-done((f32[128,896]{0,1:T(8,128)S(1)}, f32[128,896]{0,1:T(8,128)S(1)}, u32[]{:S(2)}, u32[]{:S(2)}) %collective-permute-start.5) | collective-permute-done | bytes 458784 | tf_op jit(solution)/shard_map/ppermute | solution.py:12
  337.8 11.7 %cholesky.260 = f32[128,128]{1,0:T(8,128)S(1)} custom-call(f32[128,128]{1,0:T(8,128)S(1)} %fusion.93), custom_call_target="Cholesky" | custom-call | tf_op jit(solution)/shard_map/jit(cholesky)/cholesky | solution.py:29
  350.9 9.8 %custom-call.61 = f32[1,128,128]{1,2,0:T(8,128)S(1)} custom-call(f32[1,128,128]{2,1,0:T(8,128)S(1)} %fusion.67), custom_call_target="InvertDiagBlocksLowerTriangular" | custom-call | tf_op jit(solution)/shard_map/triangular_solve/custom-call.2 | solution.py:17
  361.9 11.7 %cholesky.271 = f32[128,128]{1,0:T(8,128)S(1)} custom-call(f32[128,128]{1,0:T(8,128)S(1)} %fusion.90), custom_call_target="Cholesky" | custom-call | tf_op jit(solution)/shard_map/jit(cholesky)/cholesky | solution.py:31
  374.9 9.9 %custom-call.41 = f32[1,128,128]{1,2,0:T(8,128)S(1)} custom-call(f32[1,128,128]{2,1,0:T(8,128)S(1)} %fusion.68), custom_call_target="InvertDiagBlocksLowerTriangular" | custom-call | tf_op jit(solution)/shard_map/triangular_solve | solution.py:17
  391.3 10.2 %collective-permute-done.6 = f32[128,768]{0,1:T(8,128)S(1)} collective-permute-done((f32[128,768]{0,1:T(8,128)S(1)}, f32[128,768]{0,1:T(8,128)S(1)}, u32[]{:S(2)}, u32[]{:S(2)}) %collective-permute-start.6) | collective-permute-done | bytes 393248 | tf_op jit(solution)/shard_map/ppermute | solution.py:12
  403.5 20.3 %collective-permute-done.7 = f32[128,768]{0,1:T(8,128)S(1)} collective-permute-done((f32[128,768]{0,1:T(8,128)S(1)}, f32[128,768]{0,1:T(8,128)S(1)}, u32[]{:S(2)}, u32[]{:S(2)}) %collective-permute-start.7) | collective-permute-done | bytes 393248 | tf_op jit(solution)/shard_map/ppermute | solution.py:12
  423.8 4.3 collective-permute-start.8
  428.2 35.9 %collective-permute-done.8 = f32[128,768]{0,1:T(8,128)S(1)} collective-permute-done((f32[128,768]{0,1:T(8,128)S(1)}, f32[128,768]{0,1:T(8,128)S(1)}, u32[]{:S(2)}, u32[]{:S(2)}) %collective-permute-start.8) | collective-permute-done | bytes 393248 | tf_op jit(solution)/shard_map/ppermute | solution.py:12
  464.9 19.1 %collective-permute-start.9 = (f32[128,768]{0,1:T(8,128)}, f32[128,768]{0,1:T(8,128)}, u32[]{:S(2)}, u32[]{:S(2)}) collective-permute-start(f32[128,768]{0,1:T(8,128)} %add.136), channel_id=1, source_target_pairs={{0,256},{32,288},{64,320},{96,352},{128,384},{160,416},{192,448},{... | collective-permute-start | bytes 1179656 | tf_op jit(solution)/shard_map/ppermute | solution.py:12
  484.0 14.5 %collective-permute-done.9 = f32[128,768]{0,1:T(8,128)} collective-permute-done((f32[128,768]{0,1:T(8,128)}, f32[128,768]{0,1:T(8,128)}, u32[]{:S(2)}, u32[]{:S(2)}) %collective-permute-start.9) | collective-permute-done | bytes 393248 | tf_op jit(solution)/shard_map/ppermute | solution.py:12
  504.1 13.2 %cholesky.282 = f32[128,128]{1,0:T(8,128)} custom-call(f32[128,128]{1,0:T(8,128)} %fusion.86), custom_call_target="Cholesky" | custom-call | tf_op jit(solution)/shard_map/jit(cholesky)/cholesky | solution.py:29
  520.9 11.3 %custom-call.63 = f32[1,128,128]{1,2,0:T(8,128)} custom-call(f32[1,128,128]{2,1,0:T(8,128)} %fusion.69), custom_call_target="InvertDiagBlocksLowerTriangular" | custom-call | tf_op jit(solution)/shard_map/triangular_solve/custom-call.2 | solution.py:17
  540.3 13.2 %cholesky.293 = f32[128,128]{1,0:T(8,128)} custom-call(f32[128,128]{1,0:T(8,128)} %fusion.83), custom_call_target="Cholesky" | custom-call | tf_op jit(solution)/shard_map/jit(cholesky)/cholesky | solution.py:31
  557.1 11.6 %custom-call.42 = f32[1,128,128]{1,2,0:T(8,128)} custom-call(f32[1,128,128]{2,1,0:T(8,128)} %fusion.70), custom_call_target="InvertDiagBlocksLowerTriangular" | custom-call | tf_op jit(solution)/shard_map/triangular_solve | solution.py:17
  576.2 98.2 %all-gather.3.cloned.1.call-done = f32[2048,640]{0,1:T(8,128)} async-done(((f32[128,640]{0,1:T(8,128)}), f32[2048,640]{0,1:T(8,128)}) %all-gather.3.cloned.1.call-update) | async-done | bytes 5242896 | tf_op jit(solution)/shard_map/all_gather | solution.py:89
  674.4 3.7 copy.45
  678.9 15.3 %collective-permute-start.10 = (f32[128,640]{0,1:T(8,128)S(1)}, f32[128,640]{0,1:T(8,128)S(1)}, u32[]{:S(2)}, u32[]{:S(2)}) collective-permute-start(f32[128,640]{0,1:T(8,128)S(1)} %bitcast_reduce_fusion), channel_id=1, source_target_pairs={{0,1},{1,0},{2,3},{3,2},{4,5},{5,4},{6,7},{7,6},{8,9},{9,8},{10,11... | collective-permute-start | bytes 983048 | tf_op jit(solution)/shard_map/ppermute | solution.py:12
  695.6 11.7 %cholesky.304 = f32[128,128]{1,0:T(8,128)S(1)} custom-call(f32[128,128]{1,0:T(8,128)S(1)} %fusion.79), custom_call_target="Cholesky" | custom-call | tf_op jit(solution)/shard_map/jit(cholesky)/cholesky | solution.py:29
  708.7 9.8 %custom-call.65 = f32[1,128,128]{1,2,0:T(8,128)S(1)} custom-call(f32[1,128,128]{2,1,0:T(8,128)S(1)} %fusion.71), custom_call_target="InvertDiagBlocksLowerTriangular" | custom-call | tf_op jit(solution)/shard_map/triangular_solve/custom-call.2 | solution.py:17
  719.6 11.7 %cholesky.315 = f32[128,128]{1,0:T(8,128)S(1)} custom-call(f32[128,128]{1,0:T(8,128)S(1)} %fusion.76), custom_call_target="Cholesky" | custom-call | tf_op jit(solution)/shard_map/jit(cholesky)/cholesky | solution.py:31
  732.6 10.0 %custom-call.43 = f32[1,128,128]{1,2,0:T(8,128)S(1)} custom-call(f32[1,128,128]{2,1,0:T(8,128)S(1)} %fusion.72), custom_call_target="InvertDiagBlocksLowerTriangular" | custom-call | tf_op jit(solution)/shard_map/triangular_solve | solution.py:17
  744.0 2.7 add_convert_fusion.4
  (148 shorter events, 86.5 us)
Async XLA Ops:
  6.5 667.8 %all-gather.3.cloned.1.call-start = ((), (), s32[]{:S(2)}) async-start(), calls=%async_computation | async-start | bytes 5570560 | tf_op jit(solution)/shard_map/all_gather | solution.py:89
  14.8 0.8 copy-start.5
  71.1 2.0 copy-start
  73.1 12.9 %collective-permute-start = (f32[128,1152]{0,1:T(8,128)S(1)}, f32[128,1152]{0,1:T(8,128)S(1)}, u32[]{:S(2)}, u32[]{:S(2)}) collective-permute-start(f32[128,1152]{0,1:T(8,128)S(1)} %convolution_bitcast_fusion), channel_id=1, source_target_pairs={{0,32},{32,0},{64,96},{96,64},{128,160},{160,128},{192,224},{224,1... | collective-permute-start | bytes 1769480 | tf_op jit(solution)/shard_map/ppermute | solution.py:12
  146.9 3.0 copy-start.1
  149.9 1.4 copy-start.2
  151.3 11.1 %collective-permute-start.1 = (f32[128,1024]{0,1:T(8,128)S(1)}, f32[128,1024]{0,1:T(8,128)S(1)}, u32[]{:S(2)}, u32[]{:S(2)}) collective-permute-start(f32[128,1024]{0,1:T(8,128)S(1)} %convolution_bitcast_fusion.1), channel_id=1, source_target_pairs={{0,32},{32,0},{64,96},{96,64},{128,160},{160,128},{192,224},{224,1... | collective-permute-start | bytes 1572872 | tf_op jit(solution)/shard_map/ppermute | solution.py:12
  162.5 35.0 %collective-permute-start.2 = (f32[128,1024]{0,1:T(8,128)S(1)}, f32[128,1024]{0,1:T(8,128)}, u32[]{:S(2)}, u32[]{:S(2)}) collective-permute-start(f32[128,1024]{0,1:T(8,128)S(1)} %add.125), channel_id=1, source_target_pairs={{0,64},{32,96},{64,0},{96,32},{128,192},{160,224},{192,128},{224,1... | collective-permute-start | bytes 1572872 | tf_op jit(solution)/shard_map/ppermute | solution.py:12
  250.4 39.0 %copy-start.3 = (bf16[1024,896]{1,0:T(8,128)(2,1)}, bf16[1024,896]{1,0:T(8,128)(2,1)S(1)}, u32[]{:S(2)}) copy-start(bf16[1024,896]{1,0:T(8,128)(2,1)S(1)} %add_convert_fusion.1) | copy-start | bytes 5505028
  251.1 12.7 %collective-permute-start.3 = (f32[128,896]{0,1:T(8,128)S(1)}, f32[128,896]{0,1:T(8,128)S(1)}, u32[]{:S(2)}, u32[]{:S(2)}) collective-permute-start(f32[128,896]{0,1:T(8,128)S(1)} %convolution_bitcast_fusion.2), channel_id=1, source_target_pairs={{0,32},{32,0},{64,96},{96,64},{128,160},{160,128},{192,224},{224,1... | collective-permute-start | bytes 1376264 | tf_op jit(solution)/shard_map/ppermute | solution.py:12
  263.9 25.4 %collective-permute-start.4 = (f32[128,896]{0,1:T(8,128)S(1)}, f32[128,896]{0,1:T(8,128)S(1)}, u32[]{:S(2)}, u32[]{:S(2)}) collective-permute-start(f32[128,896]{0,1:T(8,128)S(1)} %add.129), channel_id=1, source_target_pairs={{0,64},{32,96},{64,0},{96,32},{128,192},{160,224},{192,128},{224,1... | collective-permute-start | bytes 1376264 | tf_op jit(solution)/shard_map/ppermute | solution.py:12
  289.4 48.3 %collective-permute-start.5 = (f32[128,896]{0,1:T(8,128)S(1)}, f32[128,896]{0,1:T(8,128)S(1)}, u32[]{:S(2)}, u32[]{:S(2)}) collective-permute-start(f32[128,896]{0,1:T(8,128)S(1)} %add.130), channel_id=1, source_target_pairs={{0,128},{32,160},{64,192},{96,224},{128,0},{160,32},{192,64},{224,... | collective-permute-start | bytes 1376264 | tf_op jit(solution)/shard_map/ppermute | solution.py:12
  389.4 12.1 %collective-permute-start.6 = (f32[128,768]{0,1:T(8,128)S(1)}, f32[128,768]{0,1:T(8,128)S(1)}, u32[]{:S(2)}, u32[]{:S(2)}) collective-permute-start(f32[128,768]{0,1:T(8,128)S(1)} %convolution_bitcast_fusion.3), channel_id=1, source_target_pairs={{0,32},{32,0},{64,96},{96,64},{128,160},{160,128},{192,224},{224,1... | collective-permute-start | bytes 1179656 | tf_op jit(solution)/shard_map/ppermute | solution.py:12
  401.5 22.2 %collective-permute-start.7 = (f32[128,768]{0,1:T(8,128)S(1)}, f32[128,768]{0,1:T(8,128)S(1)}, u32[]{:S(2)}, u32[]{:S(2)}) collective-permute-start(f32[128,768]{0,1:T(8,128)S(1)} %add.134), channel_id=1, source_target_pairs={{0,64},{32,96},{64,0},{96,32},{128,192},{160,224},{192,128},{224,1... | collective-permute-start | bytes 1179656 | tf_op jit(solution)/shard_map/ppermute | solution.py:12
  423.8 40.2 %collective-permute-start.8 = (f32[128,768]{0,1:T(8,128)S(1)}, f32[128,768]{0,1:T(8,128)S(1)}, u32[]{:S(2)}, u32[]{:S(2)}) collective-permute-start(f32[128,768]{0,1:T(8,128)S(1)} %add.135), channel_id=1, source_target_pairs={{0,128},{32,160},{64,192},{96,224},{128,0},{160,32},{192,64},{224,... | collective-permute-start | bytes 1179656 | tf_op jit(solution)/shard_map/ppermute | solution.py:12
  464.9 33.7 %collective-permute-start.9 = (f32[128,768]{0,1:T(8,128)}, f32[128,768]{0,1:T(8,128)}, u32[]{:S(2)}, u32[]{:S(2)}) collective-permute-start(f32[128,768]{0,1:T(8,128)} %add.136), channel_id=1, source_target_pairs={{0,256},{32,288},{64,320},{96,352},{128,384},{160,416},{192,448},{... | collective-permute-start | bytes 1179656 | tf_op jit(solution)/shard_map/ppermute | solution.py:12
  573.8 1.1 copy-start.4
  678.9 16.5 %collective-permute-start.10 = (f32[128,640]{0,1:T(8,128)S(1)}, f32[128,640]{0,1:T(8,128)S(1)}, u32[]{:S(2)}, u32[]{:S(2)}) collective-permute-start(f32[128,640]{0,1:T(8,128)S(1)} %bitcast_reduce_fusion), channel_id=1, source_target_pairs={{0,1},{1,0},{2,3},{3,2},{4,5},{5,4},{6,7},{7,6},{8,9},{9,8},{10,11... | collective-permute-start | bytes 983048 | tf_op jit(solution)/shard_map/ppermute | solution.py:12
Sparse Core Ops, SparseCore 0:
  576.3 98.0 all-gather.2
